TPU v7x, 256 devices: a whole 4x4x8 slice. The times are simulated.
256 devices in a mesh: row: 8 (over z_hi, y), col: 16 (over x, z_lo), rep: 2 (over core).
Axes of the slice: x: 4, y: 4, z: 8 (z_hi: 2, z_lo: 4; z = z_hi * 4 + z_lo), core: 2. Of those that a mesh axis runs over, the one named last changes fastest.
Arguments:
- ancestor_inverse: float32 [16384, 16384], P('row', 'col'), may hold values from -6 to 6
- tile_structure: int32 [128, 128], P('row', 'col'), may hold values from 0 to 1, as said below
- factor: float32 [16384, 512], P(('row', 'col')), may hold values from -0.046875 to 0.046875
- factor_normalizer: float32 [512, 512], replicated, may hold values from -1 to 1, as said below
- pivot_inverse: float32 [512, 512], P(None, 'rep'), may hold values from -6 to 6, as said below
Outputs:
- ancestor_columns: float32 [16384, 512], P(('row', 'col'), 'rep')
- diag_block: float32 [512, 512], P(None, 'rep')
Inputs may be any that keep to these rules, and one draw needn't show every extreme that they name: `tile_structure`: symmetric, with ones on the diagonal. `factor_normalizer`: lower triangular with ones on its diagonal. `pivot_inverse`: symmetric.
All inputs are finite; a program needn't handle non-finite values.
Results may differ from a plain program's by a relative error of at most 0.000078.
Values sent between devices are 32-bit elements; how exact they have to be, the bound alone decides.
A program may use at most 64 MiB of HBM per device.

v0:
```python
import jax
import jax.numpy as jnp
from jax import lax
from jax.sharding import PartitionSpec as P


def spread(block, axis, owner):
    block = jnp.where(lax.axis_index(axis) == owner, block, jnp.zeros_like(block))
    return lax.psum(block, axis)


def partner(block, axis, distance):
    count = lax.axis_size(axis)
    route = []
    for low in range(count):
        high = low | 1 << distance
        if high != low and high < count:
            route += [(low, high), (high, low)]
    return lax.ppermute(block, axis, route)


def contract_rows(left, right):
    return lax.dot_general(
        left,
        right,
        (((0,), (0,)), ((), ())),
        precision=lax.Precision.HIGHEST,
        preferred_element_type=jnp.float32,
    )


def body(ancestor_inverse, tile_structure, factor, factor_normalizer, pivot_inverse):
    tile_rows = factor.shape[0]
    half_width = pivot_inverse.shape[1]
    copy_index = lax.axis_index("rep")
    column_index = lax.axis_index("col")
    row_count = lax.axis_size("row")
    column_count = lax.axis_size("col")
    column_ratio = column_count // row_count
    block_rows = tile_rows * row_count
    normed = jnp.dot(
        factor,
        factor_normalizer,
        precision=lax.Precision.HIGHEST,
        preferred_element_type=jnp.float32,
    )
    own_columns = lax.dynamic_slice_in_dim(normed, copy_index * half_width, half_width, 1)
    gathered = lax.all_gather(own_columns, "col", axis=0, tiled=True)
    shared = spread(gathered, "row", column_index // column_ratio)
    column_block = lax.dynamic_slice_in_dim(
        shared, column_index % column_ratio * block_rows, block_rows, 0
    )
    tile_marks = tile_structure.astype(jnp.float32)
    across = ancestor_inverse.shape[1] // tile_rows
    masked = (
        ancestor_inverse.reshape(
            tile_rows * lax.axis_size("col") // tile_rows, tile_rows, across, tile_rows
        )
        * tile_marks[:, None, :, None]
    ).reshape(tile_rows * lax.axis_size("col"), across * tile_rows)
    ancestor_columns = lax.psum_scatter(
        -jnp.dot(
            masked,
            column_block,
            precision=lax.Precision.HIGHEST,
            preferred_element_type=jnp.float32,
        ),
        "col",
        scatter_dimension=0,
        tiled=True,
    )
    coupling_term = contract_rows(normed, ancestor_columns)
    coupling = lax.psum(coupling_term, ("row", "col"))
    outgoing_rows = lax.dynamic_slice_in_dim(coupling, (1 - copy_index) * half_width, half_width, 0)
    incoming = partner(outgoing_rows, "rep", 0)
    own_block = lax.dynamic_slice_in_dim(coupling, copy_index * half_width, half_width, 0)
    mirrored = jnp.where(
        copy_index == 0,
        jnp.concatenate([own_block, incoming], 1),
        jnp.concatenate([incoming, own_block], 1),
    )
    diag_block = pivot_inverse - 0.5 * (coupling + mirrored.T)
    return (ancestor_columns, diag_block)


def solution(mesh):
    return jax.shard_map(
        body,
        mesh=mesh,
        in_specs=(P("row", "col"), P("row", "col"), P(("row", "col"), None), P(), P(None, "rep")),
        out_specs=(P(("row", "col"), "rep"), P(None, "rep")),
        check_vma=False,
    )
```

profile of v0, /device:TPU:1, one launch (start us, length us, event | category | flops | bytes accessed | tf_op | source)
XLA Modules:
  0.0 569.2 jit_solution(9534586514955601280)
XLA Ops:
  7.2 0.0 copy-start
  7.2 0.0 all-gather.2.cloned.1.call-start
  7.2 1.2 copy-done
  8.4 1.7 fusion.9
  10.1 0.7 constant_dynamic-slice_fusion.2
  10.7 0.0 all-gather.2.cloned.1.call-update
  10.8 0.0 all-reduce.3.cloned.1.call-start
  10.8 82.3 %all-gather.2.cloned.1.call-done = f32[2048,256]{1,0:T(8,128)} async-done(((f32[128,256]{1,0:T(8,128)}), f32[2048,256]{1,0:T(8,128)}) %all-gather.2.cloned.1.call-update) | async-done | bytes 2097168 | tf_op jit(solution)/shard_map/all_gather | solution.py:48
  93.1 3.1 broadcast_select_fusion
  96.2 0.0 copy-start.4
  96.2 0.0 all-reduce.3.cloned.1.call-update
  96.2 0.0 reduce-scatter.2.cloned.1.call-start
  96.3 0.6 copy-done.4
  96.9 0.1 copy.7
  96.9 138.5 %all-reduce.3.cloned.1.call-done = f32[2048,256]{1,0:T(8,128)} async-done(((f32[2048,256]{1,0:T(8,128)}), f32[2048,256]{1,0:T(8,128)}) %all-reduce.3.cloned.1.call-update) | async-done | bytes 2097168 | tf_op jit(solution)/shard_map/psum | solution.py:9
  235.4 0.0 copy-start.2
  235.4 0.6 mul.27
  236.0 1.0 copy-done.2
  237.0 10.5 %fusion.2 = f32[2048,256]{1,0:T(8,128)} fusion(f32[2048,1024]{1,0:T(8,128)} %param.5, f32[256,8,8,128]{3,2,1,0:T(8,128)S(1)} %bitcast.19, f32[2048,256]{1,0:T(8,128)S(1)} %copy-done.2, s32[]{:T(128)S(6)} %select_n.42), kind=kOutput, calls=%fused_computation.3 | convolution fusion | flops 6445072384 | bytes 19922948 | tf_op jit(solution)/shard_map/dot_general | solution.py:62
  247.5 0.0 reduce-scatter.2.cloned.1.call-update
  247.6 0.0 copy-start.3
  247.6 0.0 all-reduce.5.cloned.1.call-start
  247.6 81.7 %reduce-scatter.2.cloned.1.call-done = f32[128,256]{1,0:T(8,128)} async-done(((f32[2048,256]{1,0:T(8,128)}), f32[128,256]{1,0:T(8,128)}) %reduce-scatter.2.cloned.1.call-update) | async-done | bytes 131088 | tf_op jit(solution)/shard_map/reduce_scatter | solution.py:61
  329.3 2.3 fusion.10
  331.6 0.0 all-reduce.5.cloned.1.call-update
  331.7 222.4 %all-reduce.5.cloned.1.call-done = f32[512,256]{1,0:T(8,128)} async-done(((f32[512,256]{1,0:T(8,128)}), f32[512,256]{1,0:T(8,128)}) %all-reduce.5.cloned.1.call-update) | async-done | bytes 524304 | tf_op jit(solution)/shard_map/psum | solution.py:73
  554.0 0.0 copy-start.1
  554.0 1.1 constant_dynamic-slice_fusion.1
  555.1 0.1 copy.11
  555.3 5.3 collective-permute-start
  560.6 0.1 copy.10
  560.7 1.0 collective-permute-done
  561.7 0.0 copy-done.3
  561.7 0.0 copy-done.1
  561.7 0.9 fusion.7
  (1 shorter events, 0.0 us)
Async XLA Ops:
  7.2 1.2 copy-start
  7.2 85.9 %all-gather.2.cloned.1.call-start = ((), (), s32[]{:S(2)}) async-start(), calls=%async_computation.1 | async-start | bytes 2228224 | tf_op jit(solution)/shard_map/all_gather | solution.py:48
  10.8 224.7 %all-reduce.3.cloned.1.call-start = ((), (), s32[]{:S(2)}) async-start(), calls=%async_computation.2 | async-start | bytes 4194304 | tf_op jit(solution)/shard_map/psum | solution.py:9
  96.2 0.7 copy-start.4
  96.2 233.1 %reduce-scatter.2.cloned.1.call-start = ((), (), s32[]{:S(2)}) async-start(), calls=%async_computation.3 | async-start | bytes 2228224 | tf_op jit(solution)/shard_map/reduce_scatter | solution.py:61
  235.4 1.6 copy-start.2
  247.6 314.2 %copy-start.3 = (f32[512,256]{1,0:T(8,128)S(1)}, f32[512,256]{1,0:T(8,128)}, u32[]{:S(2)}) copy-start(f32[512,256]{1,0:T(8,128)} %param.9) | copy-start | bytes 1572868
  247.6 306.4 %all-reduce.5.cloned.1.call-start = ((), (), s32[]{:S(2)}) async-start(), calls=%async_computation.4 | async-start | bytes 1048576 | tf_op jit(solution)/shard_map/psum | solution.py:73
  554.0 7.7 %copy-start.1 = (f32[512,256]{1,0:T(8,128)S(1)}, f32[512,256]{1,0:T(8,128)}, u32[]{:S(2)}) copy-start(f32[512,256]{1,0:T(8,128)} %all-reduce.5.cloned.1.call-done) | copy-start | bytes 1572868
  555.3 6.4 %collective-permute-start = (f32[256,256]{0,1:T(8,128)S(1)}, f32[256,256]{0,1:T(8,128)S(1)}, u32[]{:S(2)}, u32[]{:S(2)}) collective-permute-start(f32[256,256]{0,1:T(8,128)S(1)} %copy.11), channel_id=1, source_target_pairs={{0,1},{1,0},{2,3},{3,2},{4,5},{5,4},{6,7},{7,6},{8,9},{9,8},{10,11... | collective-permute-start | bytes 786440 | tf_op jit(solution)/shard_map/ppermute | solution.py:19
Sparse Core Ops, SparseCore 0:
  10.9 82.1 all-gather.1
  96.3 139.0 all-reduce.2
  247.7 81.5 reduce-scatter.1
  335.2 218.8 all-reduce.4
where the time goes:
time: 569 us
  waiting for transfers between devices  526 us (92%)
  matrix products  14.5 us (3%)
  between operations  13.9 us (2%)
    psum x1, waiting for transfers between devices, body(): coupling = lax.psum(coupling_term, ('row', 'col'))  222 us
    psum x1, waiting for transfers between devices, spread(): return lax.psum(block, axis)  138 us
    all_gather x1, waiting for transfers between devices, body(): gathered = lax.all_gather(own_columns, 'col', axis=0, tiled=True)  82.3 us
    reduce_scatter x1, waiting for transfers between devices, body(): lax.psum_scatter(-jnp.dot(masked, column_block, precision=lax.Precision.H...  81.7 us
  transfers between devices with their start and end apart: 5, of which 5 were waited for; matrix products, arithmetic and copies ran while one was open for 0% of the time, Pallas kernels for 0%

commit v1 on v0

v1 whole, which is shorter than its diff:
```python
import jax
import jax.numpy as jnp
from jax import lax
from jax.experimental import pallas as pl
from jax.experimental.pallas import tpu as pltpu
from jax.sharding import PartitionSpec as P

F32 = jnp.float32
BF16 = jnp.bfloat16
MESH = pl.DeviceIdType.MESH


def split(value):
    high = value.astype(BF16)
    return high, (value - high.astype(F32)).astype(BF16)


def dot(left, right):
    return jnp.dot(left, right, preferred_element_type=F32)


def dot3(left, right):
    lh, ll = left
    rh, rl = right
    return dot(lh, rh) + (dot(lh, rl) + dot(ll, rh))


def kernel(
    tiles, a_hbm, f_hbm, n_hbm, y_out, s_out,
    af, ah, al, fac, nrm, nown, nth, ntl, xf, xc, p, gin, rin, zc, zin, yb, cp, win, tv, uin, cf, ein,
    a_sem, i_sem, s1s, s1r, ys, yr, xs, xr, zs, zr, ws, wr, us, ur, gs, gr, es, er,
):
    row, col, rep = (lax.axis_index(name) for name in ("row", "col", "rep"))
    tile, width = fac.shape
    half = width // 2
    part = half // 2
    quad = 4 * tile
    chunk = width // 16
    x, z_lo, z_hi, y = col // 4, col % 4, row // 4, row % 4
    z = z_hi * 4 + z_lo
    sent = []

    def place(px, py, pz):
        return (pz // 4 * 4 + py, px * 4 + pz % 4, rep)

    def send(src, dst, send_sem, recv_sem, device):
        copy = pltpu.make_async_remote_copy(
            src_ref=src, dst_ref=dst, send_sem=send_sem, recv_sem=recv_sem,
            device_id=device, device_id_type=MESH,
        )
        copy.start()
        sent.append(copy)

    def arrived(dst, sem):
        pltpu.make_async_copy(dst, dst, sem).wait()

    load_f = pltpu.make_async_copy(f_hbm, fac, i_sem.at[0])
    load_n = pltpu.make_async_copy(n_hbm, nrm, i_sem.at[1])
    load_f.start()
    load_n.start()

    def rows_of(a):
        return pl.ds(pl.multiple_of(a * tile, tile), tile)

    for a in range(16):
        pltpu.make_async_copy(a_hbm.at[rows_of(a)], af.at[rows_of(a)], a_sem.at[a]).start()

    barrier = pltpu.get_barrier_semaphore()
    for dx in range(4):
        for dy in range(4):
            if dx or dy:
                pl.semaphore_signal(barrier, inc=1, device_id=place((x + dx) % 4, (y + dy) % 4, z), device_id_type=MESH)
    for dz in range(1, 8):
        pl.semaphore_signal(barrier, inc=1, device_id=place(x, y, (z + dz) % 8), device_id_type=MESH)
    pl.semaphore_signal(barrier, inc=1, device_id=(row, col, 1 - rep), device_id_type=MESH)
    for slot in range(2):
        from_row, from_col = col // 2, col % 2 * 8 + y * 2 + slot
        mine = jnp.logical_and(from_row == row, from_col == col)

        @pl.when(jnp.logical_not(mine))
        def _():
            pl.semaphore_signal(barrier, inc=1, device_id=(from_row, from_col, rep), device_id_type=MESH)

    load_f.wait()
    load_n.wait()
    normed = dot3(split(fac[...]), split(nrm[...]))
    fac[...] = normed
    for q in range(2):
        nown[q] = fac[:, pl.ds(pl.multiple_of(rep * half + q * part, part), part)]

    kth = col % 8
    to_col = 2 * row + col // 8
    stays = jnp.logical_and(to_col == col, kth // 2 == y)
    pl.semaphore_wait(barrier, 15 + 7 + 1 + 2 - stays.astype(jnp.int32))
    landing = pl.ds(pl.multiple_of(kth * tile, tile), tile)
    first = []
    for q in range(2):
        for zh in range(2):
            to_row = zh * 4 + kth // 2
            mine = jnp.logical_and(to_row == row, to_col == col)
            copy = pltpu.make_async_remote_copy(
                src_ref=nown.at[q], dst_ref=xf.at[q, landing], send_sem=s1s.at[q, zh], recv_sem=s1r.at[q, kth % 2],
                device_id=(to_row, to_col, rep), device_id_type=MESH,
            )
            first.append((copy, mine))

            @pl.when(jnp.logical_not(mine))
            def _():
                copy.start()

            @pl.when(mine)
            def _():
                pltpu.make_async_copy(nown.at[q], xf.at[q, landing], s1r.at[q, kth % 2]).start()

    def mask_rows(a, carry):
        pltpu.make_async_copy(a_hbm.at[rows_of(a)], af.at[rows_of(a)], a_sem.at[a]).wait()
        for b in range(8):
            columns = slice(b * tile, (b + 1) * tile)
            high, low = split(af[rows_of(a), columns] * tiles[a, b].astype(F32))
            ah[rows_of(a), columns] = high
            al[rows_of(a), columns] = low
        return carry

    def y_exchange(q):
        for slot in range(2):
            arrived(xf.at[q, rows_of(y * 2 + slot)], s1r.at[q, slot])
        pair = pl.ds(pl.multiple_of(y * 2 * tile, 2 * tile), 2 * tile)
        for dy in (1, 3, 2):
            send(xf.at[q, pair], xf.at[q, pair], ys.at[q, dy - 1], yr.at[q, dy - 1], place(x, (y + dy) % 4, z))

    transposed = fac[...].T
    nth[...], ntl[...] = split(transposed)
    lax.fori_loop(0, 4, mask_rows, 0)
    y_exchange(0)
    lax.fori_loop(4, 8, mask_rows, 0)
    y_exchange(1)
    lax.fori_loop(8, 16, mask_rows, 0)

    def x_ready(q):
        for dy in range(1, 4):
            pair = pl.ds(pl.multiple_of((y + 4 - dy) % 4 * 2 * tile, 2 * tile), 2 * tile)
            arrived(xf.at[q, pair], yr.at[q, dy - 1])
        high, low = split(xf[q])
        xc[q, :, :part] = high
        xc[q, :, part:] = low

    xp, xo, xm = (x + 1) % 4, (x + 2) % 4, (x + 3) % 4

    def piece(block, side):
        return pl.ds(pl.multiple_of(block * quad + side * 2 * tile, 2 * tile), 2 * tile)

    sides = [slice(0, 2 * tile), slice(2 * tile, quad)]

    def product(q, block, side):
        rows = piece(block, side)
        both = dot(ah[rows, :], xc[q])
        p[q, rows, :] = both[:, :part] + (both[:, part:] + dot(al[rows, :], xc[q, :, :part]))

    def x_send(q, index, block, side, target, dst):
        send(p.at[q, piece(block, side)], dst, xs.at[q, index], xr.at[q, index], place(target, y, z))

    def products(q):
        x_ready(q)
        product(q, xo, 0)
        x_send(q, 0, xo, 0, xp, gin.at[q, 0])
        product(q, xo, 1)
        x_send(q, 1, xo, 1, xm, gin.at[q, 1])
        product(q, xp, 1)
        x_send(q, 2, xp, 1, xp, rin.at[q, 0, sides[1]])
        product(q, xm, 0)
        x_send(q, 3, xm, 0, xm, rin.at[q, 1, sides[0]])
        product(q, xp, 0)
        product(q, xm, 1)
        product(q, x, 0)
        product(q, x, 1)

    def x_pass_on(q):
        arrived(gin.at[q, 0], xr.at[q, 0])
        p[q, piece(xp, 0), :] += gin[q, 0]
        x_send(q, 4, xp, 0, xp, rin.at[q, 0, sides[0]])
        arrived(gin.at[q, 1], xr.at[q, 1])
        p[q, piece(xm, 1), :] += gin[q, 1]
        x_send(q, 5, xm, 1, xm, rin.at[q, 1, sides[1]])

    def z_send(q):
        arrived(rin.at[q, 0, sides[1]], xr.at[q, 2])
        arrived(rin.at[q, 1, sides[0]], xr.at[q, 3])
        arrived(rin.at[q, 0, sides[0]], xr.at[q, 4])
        arrived(rin.at[q, 1, sides[1]], xr.at[q, 5])
        for side in range(2):
            zc[q, sides[side]] = p[q, piece(x, side), :] + (rin[q, 0, sides[side]] + rin[q, 1, sides[side]])
        for dz in (2, 1, 3):
            to = (z_lo + dz) % 4
            send(zc.at[q, rows_of(to)], zin.at[q, dz - 1], zs.at[q, dz - 1], zr.at[q, dz - 1], place(x, y, z_hi * 4 + to))

    def plane():
        return [(dx, dy, dx * 4 + dy - 1) for dx in range(4) for dy in range(4) if dx or dy]

    def chunk_rows(index):
        return pl.ds(pl.multiple_of(index * chunk, chunk), chunk)

    def couple(q):
        total = zc[q, rows_of(z_lo), :]
        for dz in range(1, 4):
            arrived(zin.at[q, dz - 1], zr.at[q, dz - 1])
            total += zin[q, dz - 1]
        total = -total
        y_out[:, q * part : (q + 1) * part] = total
        cp[q] = dot3((nth[...], ntl[...]), split(total))
        for dx, dy, slot in plane():
            tx, ty = (x + dx) % 4, (y + dy) % 4
            send(cp.at[q, chunk_rows(tx * 4 + ty)], win.at[q, slot], ws.at[q, slot], wr.at[q, slot], place(tx, ty, z))

    own = x * 4 + y

    def z_share(q):
        total = cp[q, chunk_rows(own), :]
        for _, _, slot in plane():
            arrived(win.at[q, slot], wr.at[q, slot])
            total += win[q, slot]
        uin[q, z] = total
        tv[q] = total
        for dz in (4, 3, 5, 2, 6, 1, 7):
            send(tv.at[q], uin.at[q, z], us.at[q, dz - 1], ur.at[q, z], place(x, y, (z + dz) % 8))

    def gather(q):
        for dz in range(1, 8):
            source = (z + dz) % 8
            arrived(uin.at[q, source], ur.at[q, source])
        total = uin[q, 0]
        for source in range(1, 8):
            total += uin[q, source]
        cf[q, chunk_rows(own), :] = total
        for dx, dy, slot in plane():
            to = place((x + dx) % 4, (y + dy) % 4, z)
            send(cf.at[q, chunk_rows(own)], cf.at[q, chunk_rows(own)], gs.at[q, slot], gr.at[q, slot], to)

    mine_rows = pl.ds(pl.multiple_of(rep * half, half), half)
    other_rows = pl.ds(pl.multiple_of((1 - rep) * half, half), half)

    def exchange(q):
        for dx, dy, slot in plane():
            source = (x + 4 - dx) % 4 * 4 + (y + 4 - dy) % 4
            arrived(cf.at[q, chunk_rows(source)], gr.at[q, slot])
        send(cf.at[q, other_rows], ein.at[q], es.at[q], er.at[q], (row, col, 1 - rep))

    products(0)
    x_pass_on(0)
    products(1)
    z_send(0)
    x_pass_on(1)
    couple(0)
    z_send(1)
    z_share(0)
    couple(1)
    gather(0)
    z_share(1)
    gather(1)
    exchange(0)
    exchange(1)
    block = jnp.concatenate([cf[0, mine_rows, :], cf[1, mine_rows, :]], 1)
    s_out[mine_rows, :] = 0.5 * (block + block.T)
    for q in range(2):
        arrived(ein.at[q], er.at[q])
    mirrored = jnp.concatenate([ein[0].T, ein[1].T], 0)
    s_out[other_rows, :] = 0.5 * (jnp.concatenate([cf[0, other_rows, :], cf[1, other_rows, :]], 1) + mirrored)
    for copy, mine in first:

        @pl.when(jnp.logical_not(mine))
        def _():
            copy.wait_send()

    for copy in sent:
        copy.wait_send()


def body(ancestor_inverse, tile_structure, factor, factor_normalizer, pivot_inverse):
    tile, width = factor.shape
    part = width // 4
    rows, columns = ancestor_inverse.shape
    chunk = width // 16
    vmem, dma = pltpu.VMEM, pltpu.SemaphoreType.DMA
    anywhere = pl.BlockSpec(memory_space=pl.ANY)
    in_vmem = pl.BlockSpec(memory_space=pltpu.VMEM)
    ancestor_columns, symmetric = pl.pallas_call(
        kernel,
        out_shape=(
            jax.ShapeDtypeStruct((tile, 2 * part), F32),
            jax.ShapeDtypeStruct((width, 2 * part), F32),
        ),
        in_specs=[pl.BlockSpec(memory_space=pltpu.SMEM), anywhere, anywhere, anywhere],
        out_specs=(in_vmem, in_vmem),
        scratch_shapes=[
            vmem((rows, columns), F32),
            vmem((rows, columns), BF16),
            vmem((rows, columns), BF16),
            vmem((tile, width), F32),
            vmem((width, width), F32),
            vmem((2, tile, part), F32),
            vmem((width, tile), BF16),
            vmem((width, tile), BF16),
            vmem((2, columns, part), F32),
            vmem((2, columns, 2 * part), BF16),
            vmem((2, rows, part), F32),
            vmem((2, 2, 2 * tile, part), F32),
            vmem((2, 2, 4 * tile, part), F32),
            vmem((2, 4 * tile, part), F32),
            vmem((2, 3, tile, part), F32),
            vmem((2, tile, part), F32),
            vmem((2, width, part), F32),
            vmem((2, 15, chunk, part), F32),
            vmem((2, chunk, part), F32),
            vmem((2, 8, chunk, part), F32),
            vmem((2, width, part), F32),
            vmem((2, 2 * part, part), F32),
            dma((16,)),
            dma((2,)),
            dma((2, 2)),
            dma((2, 2)),
            dma((2, 3)),
            dma((2, 3)),
            dma((2, 6)),
            dma((2, 6)),
            dma((2, 3)),
            dma((2, 3)),
            dma((2, 15)),
            dma((2, 15)),
            dma((2, 7)),
            dma((2, 8)),
            dma((2, 15)),
            dma((2, 15)),
            dma((2,)),
            dma((2,)),
        ],
        compiler_params=pltpu.CompilerParams(collective_id=0, has_side_effects=True, vmem_limit_bytes=48 * 1024 * 1024),
    )(tile_structure, ancestor_inverse, factor, factor_normalizer)
    return ancestor_columns, pivot_inverse - symmetric


def solution(mesh):
    return jax.shard_map(
        body,
        mesh=mesh,
        in_specs=(P("row", "col"), P("row", "col"), P(("row", "col"), None), P(), P(None, "rep")),
        out_specs=(P(("row", "col"), "rep"), P(None, "rep")),
        check_vma=False,
    )
```

time: 569 us -> 99.2 us (0.17)
  waiting for transfers between devices: 526 us -> 0 us
  Pallas kernels: 0 us -> 93.9 us
  matrix products: 14.5 us -> 0 us
  between operations: 13.9 us -> 0.65 us
    psum x2 -> x0, waiting for transfers between devices: 361 us -> none  [the longest x1 222 us: body(): coupling = lax.psum(coupling_term, ('row', 'col'))]
    pallas_call x0 -> x1, Pallas kernels: none -> 93.9 us  [body(): pl.pallas_call(kernel, out_shape=(jax.ShapeDtypeStruct((tile, 2 * part),...]
    all_gather x1 -> x0, waiting for transfers between devices: 82.3 us -> none  [body(): gathered = lax.all_gather(own_columns, 'col', axis=0, tiled=True)]
    reduce_scatter x1 -> x0, waiting for transfers between devices: 81.7 us -> none  [body(): lax.psum_scatter(-jnp.dot(masked, column_block, precision=lax.Precision.H...]
    dot_general x3 -> x0, matrix products: 14.5 us -> none  [the longest x1 10.5 us: body(): jnp.dot(masked, column_block, precision=lax.Precision.HIGHEST, preferred_...]
  transfers between devices with their start and end apart: 5 -> 0, of which waited for: 5 -> 0; matrix products, arithmetic and copies ran while one was open for 0% -> 0% of each run, Pallas kernels for 0% -> 0%
where the time goes in v1:
time: 99.2 us; the launch traced here: 99 us
  Pallas kernels  93.9 us (95%)
  local copies, waits for them, and re-layouts  3.59 us (4%)
    pallas_call x1, Pallas kernels, body(): pl.pallas_call(kernel, out_shape=(jax.ShapeDtypeStruct((tile, 2 * part),...  93.9 us
    unnamed x8, local copies, waits for them, and re-layouts  3.59 us

profile of v1, /device:TPU:1, one launch (start us, length us, event | category | flops | bytes accessed | tf_op | source)
XLA Modules:
  0.0 99.0 jit_solution(6440973142556122433)
XLA Ops:
  0.6 0.8 copy.7.tiles
  1.4 0.0 copy-start
  1.4 1.2 %copy-done = f32[512,512]{1,0:T(8,128)S(1)} copy-done((f32[512,512]{1,0:T(8,128)S(1)}, f32[512,512]{1,0:T(8,128)}, u32[]{:S(2)}) %copy-start) | copy-done | bytes 1048600
  2.6 0.0 copy-start.1
  2.6 0.9 copy-done.1
  3.6 0.0 copy-start.2
  3.6 93.9 %shard_map.68 = (f32[128,256]{1,0:T(8,128)S(1)}, f32[512,256]{1,0:T(8,128)S(1)}) custom-call(s32[16,8]{1,0:T(8,128)S(1)} %copy.7.tiles, f32[2048,1024]{1,0:T(8,128)} %a_hbm.1, f32[128,512]{1,0:T(8,128)S(1)} %copy-done.1, f32[512,512]{1,0:T(8,128)S(1)} %copy-done), custom_call_target="tpu_custom_call" | custom-call | tf_op jit(solution)/shard_map/pallas_call | solution.py:285
  97.5 0.0 copy-done.2
  97.5 0.9 sub.3
  98.4 0.7 copy.9
Async XLA Ops:
  1.4 1.2 %copy-start = (f32[512,512]{1,0:T(8,128)S(1)}, f32[512,512]{1,0:T(8,128)}, u32[]{:S(2)}) copy-start(f32[512,512]{1,0:T(8,128)} %n_hbm.1) | copy-start | bytes 3145732
  2.6 0.9 copy-start.1
  3.6 93.9 %copy-start.2 = (f32[512,256]{1,0:T(8,128)S(1)}, f32[512,256]{1,0:T(8,128)}, u32[]{:S(2)}) copy-start(f32[512,256]{1,0:T(8,128)} %param.9) | copy-start | bytes 1572868

commit v2 on v1

--- a/solution.py
+++ b/solution.py
@@ -28,7 +28,7 @@
 def kernel(
     tiles, a_hbm, f_hbm, n_hbm, y_out, s_out,
     af, ah, al, fac, nrm, nown, nth, ntl, xf, xc, p, gin, rin, zc, zin, yb, cp, win, tv, uin, cf, ein,
-    a_sem, i_sem, s1s, s1r, ys, yr, xs, xr, zs, zr, ws, wr, us, ur, gs, gr, es, er,
+    bn, nz, a_sem, i_sem, bs, br, ns, nr, ms, mr, s1s, s1r, ys, yr, xs, xr, zs, zr, ws, wr, us, ur, gs, gr, es, er,
 ):
     row, col, rep = (lax.axis_index(name) for name in ("row", "col", "rep"))
     tile, width = fac.shape
@@ -55,9 +55,15 @@
         pltpu.make_async_copy(dst, dst, sem).wait()
 
     load_f = pltpu.make_async_copy(f_hbm, fac, i_sem.at[0])
-    load_n = pltpu.make_async_copy(n_hbm, nrm, i_sem.at[1])
     load_f.start()
-    load_n.start()
+    slices = [rep * 2, rep * 2 + 1, 2 - rep * 2, 3 - rep * 2]
+
+    def slice_of(index):
+        return pl.ds(pl.multiple_of(slices[index] * part, part), part)
+
+    load_n = [pltpu.make_async_copy(n_hbm.at[:, slice_of(i)], nrm.at[i], i_sem.at[1 + i]) for i in range(4)]
+    for load in load_n:
+        load.start()
 
     def rows_of(a):
         return pl.ds(pl.multiple_of(a * tile, tile), tile)
@@ -68,13 +74,14 @@
     barrier = pltpu.get_barrier_semaphore()
     for dx in range(4):
         for dy in range(4):
+            near = place((x + dx) % 4, (y + dy) % 4, z)
             if dx or dy:
-                pl.semaphore_signal(barrier, inc=1, device_id=place((x + dx) % 4, (y + dy) % 4, z), device_id_type=MESH)
+                pl.semaphore_signal(barrier, inc=1, device_id=near, device_id_type=MESH)
+            pl.semaphore_signal(barrier, inc=1, device_id=(near[0], near[1], 1 - rep), device_id_type=MESH)
     for dz in range(1, 8):
         pl.semaphore_signal(barrier, inc=1, device_id=place(x, y, (z + dz) % 8), device_id_type=MESH)
-    pl.semaphore_signal(barrier, inc=1, device_id=(row, col, 1 - rep), device_id_type=MESH)
-    for slot in range(2):
-        from_row, from_col = col // 2, col % 2 * 8 + y * 2 + slot
+    for slot in range(8):
+        from_row, from_col = row, col % 2 * 8 + slot
         mine = jnp.logical_and(from_row == row, from_col == col)
 
         @pl.when(jnp.logical_not(mine))
@@ -82,25 +89,74 @@
             pl.semaphore_signal(barrier, inc=1, device_id=(from_row, from_col, rep), device_id_type=MESH)
 
     load_f.wait()
-    load_n.wait()
-    normed = dot3(split(fac[...]), split(nrm[...]))
-    fac[...] = normed
-    for q in range(2):
-        nown[q] = fac[:, pl.ds(pl.multiple_of(rep * half + q * part, part), part)]
+
+    def normed(index):
+        load_n[index].wait()
+        value = dot3(split(fac[...]), split(nrm[index]))
+        if index < 2:
+            nown[index] = value
+        return value
+
+    def keep_transposed(index, value):
+        high, low = split(value.T)
+        nth[slice_of(index), rows_of(z_lo)] = high
+        ntl[slice_of(index), rows_of(z_lo)] = low
+
+    own_slices = pl.ds(rep * 2, 2)
+
+    def normed_share():
+        for dz in (2, 1, 3):
+            to = place(x, y, z_hi * 4 + (z_lo + dz) % 4)
+            send(nown, nz.at[z_lo, own_slices], ns.at[dz - 1], nr.at[z_lo], to)
+
+    def normed_forward():
+        for dz in range(1, 4):
+            peer = (z_lo + dz) % 4
+            arrived(nz.at[peer, own_slices], nr.at[peer])
+            send(nz.at[peer, own_slices], nz.at[peer, own_slices], ms.at[dz - 1], mr.at[peer], (row, col, 1 - rep))
+
+    def normed_ready():
+        for dz in range(1, 4):
+            peer = (z_lo + dz) % 4
+            arrived(nz.at[peer, pl.ds(2 - rep * 2, 2)], mr.at[peer])
+            for index in range(4):
+                high, low = split(nz[peer, index].T)
+                nth[index * part : (index + 1) * part, rows_of(peer)] = high
+                ntl[index * part : (index + 1) * part, rows_of(peer)] = low
+
+    value = normed(0)
 
     kth = col % 8
     to_col = 2 * row + col // 8
-    stays = jnp.logical_and(to_col == col, kth // 2 == y)
-    pl.semaphore_wait(barrier, 15 + 7 + 1 + 2 - stays.astype(jnp.int32))
-    landing = pl.ds(pl.multiple_of(kth * tile, tile), tile)
+    for ty in range(1, 4):
+        to = place(x, (y + ty) % 4, (z + 4) % 8)
+        pl.semaphore_signal(barrier, inc=1, device_id=to, device_id_type=MESH)
+    pl.semaphore_wait(barrier, 31 + 7 + 3 + 8 - (col % 2 == col // 8).astype(jnp.int32))
+    piece_rows = tile // 4
     first = []
-    for q in range(2):
+
+    def row_send(q):
         for zh in range(2):
-            to_row = zh * 4 + kth // 2
-            mine = jnp.logical_and(to_row == row, to_col == col)
+            for ty in range(4):
+                if zh or ty:
+                    to_y, to_z = (y + ty) % 4, (z + zh * 4) % 8
+                    source = nown.at[q, pl.ds(pl.multiple_of(to_y * piece_rows, piece_rows), piece_rows)]
+                    send(source, bn.at[q, row], bs.at[q, zh * 4 + ty - 1], br.at[q, row], place(x, to_y, to_z))
+        bn[q, row] = nown[q, pl.ds(pl.multiple_of(y * piece_rows, piece_rows), piece_rows)]
+
+    def plane_send(q):
+        for shift in range(8):
+            owner = (col // 2 + shift) % 8
+
+            @pl.when(owner != row)
+            def _():
+                arrived(bn.at[q, owner], br.at[q, owner])
+
+            target = 2 * owner + col // 8
+            mine = target == col
             copy = pltpu.make_async_remote_copy(
-                src_ref=nown.at[q], dst_ref=xf.at[q, landing], send_sem=s1s.at[q, zh], recv_sem=s1r.at[q, kth % 2],
-                device_id=(to_row, to_col, rep), device_id_type=MESH,
+                src_ref=bn.at[q, owner], dst_ref=xf.at[q, kth, y], send_sem=s1s.at[q, shift], recv_sem=s1r.at[q, kth],
+                device_id=(row, target, rep), device_id_type=MESH,
             )
             first.append((copy, mine))
 
@@ -110,7 +166,7 @@
 
             @pl.when(mine)
             def _():
-                pltpu.make_async_copy(nown.at[q], xf.at[q, landing], s1r.at[q, kth % 2]).start()
+                pltpu.make_async_copy(bn.at[q, owner], xf.at[q, kth, y], s1r.at[q, kth]).start()
 
     def mask_rows(a, carry):
         pltpu.make_async_copy(a_hbm.at[rows_of(a)], af.at[rows_of(a)], a_sem.at[a]).wait()
@@ -122,25 +178,29 @@
         return carry
 
     def y_exchange(q):
-        for slot in range(2):
-            arrived(xf.at[q, rows_of(y * 2 + slot)], s1r.at[q, slot])
-        pair = pl.ds(pl.multiple_of(y * 2 * tile, 2 * tile), 2 * tile)
+        for slot in range(8):
+            arrived(xf.at[q, slot, y], s1r.at[q, slot])
         for dy in (1, 3, 2):
-            send(xf.at[q, pair], xf.at[q, pair], ys.at[q, dy - 1], yr.at[q, dy - 1], place(x, (y + dy) % 4, z))
-
-    transposed = fac[...].T
-    nth[...], ntl[...] = split(transposed)
-    lax.fori_loop(0, 4, mask_rows, 0)
+            send(xf.at[q, :, y], xf.at[q, :, y], ys.at[q, dy - 1], yr.at[q, dy - 1], place(x, (y + dy) % 4, z))
+
+    row_send(0)
+    keep_transposed(0, value)
+    for index in range(1, 4):
+        keep_transposed(index, normed(index))
+    lax.fori_loop(0, 6, mask_rows, 0)
+    plane_send(0)
+    row_send(1)
+    lax.fori_loop(6, 12, mask_rows, 0)
     y_exchange(0)
-    lax.fori_loop(4, 8, mask_rows, 0)
+    lax.fori_loop(12, 16, mask_rows, 0)
+    plane_send(1)
     y_exchange(1)
-    lax.fori_loop(8, 16, mask_rows, 0)
+    normed_share()
 
     def x_ready(q):
         for dy in range(1, 4):
-            pair = pl.ds(pl.multiple_of((y + 4 - dy) % 4 * 2 * tile, 2 * tile), 2 * tile)
-            arrived(xf.at[q, pair], yr.at[q, dy - 1])
-        high, low = split(xf[q])
+            arrived(xf.at[q, :, (y + 4 - dy) % 4], yr.at[q, dy - 1])
+        high, low = split(xf[q].reshape(8 * tile, part))
         xc[q, :, :part] = high
         xc[q, :, part:] = low
 
@@ -200,16 +260,17 @@
         return pl.ds(pl.multiple_of(index * chunk, chunk), chunk)
 
     def couple(q):
+        cp[q] = dot3((nth[...], ntl[...]), split(-zc[q]))
+        for dx, dy, slot in plane():
+            tx, ty = (x + dx) % 4, (y + dy) % 4
+            send(cp.at[q, chunk_rows(tx * 4 + ty)], win.at[q, slot], ws.at[q, slot], wr.at[q, slot], place(tx, ty, z))
+
+    def columns_out(q):
         total = zc[q, rows_of(z_lo), :]
         for dz in range(1, 4):
             arrived(zin.at[q, dz - 1], zr.at[q, dz - 1])
             total += zin[q, dz - 1]
-        total = -total
-        y_out[:, q * part : (q + 1) * part] = total
-        cp[q] = dot3((nth[...], ntl[...]), split(total))
-        for dx, dy, slot in plane():
-            tx, ty = (x + dx) % 4, (y + dy) % 4
-            send(cp.at[q, chunk_rows(tx * 4 + ty)], win.at[q, slot], ws.at[q, slot], wr.at[q, slot], place(tx, ty, z))
+        y_out[:, q * part : (q + 1) * part] = -total
 
     own = x * 4 + y
 
@@ -235,33 +296,57 @@
             to = place((x + dx) % 4, (y + dy) % 4, z)
             send(cf.at[q, chunk_rows(own)], cf.at[q, chunk_rows(own)], gs.at[q, slot], gr.at[q, slot], to)
 
+        @pl.when(crosses)
+        def _():
+            for copy in cross_copies(q):
+                copy.start()
+
+    crosses = own // 8 != rep
+
+    def cross_copies(q):
+        copies = []
+        for dx in range(4):
+            for dy in range(4):
+                to = place((x + dx) % 4, (y + dy) % 4, z)
+                copies.append(
+                    pltpu.make_async_remote_copy(
+                        src_ref=cf.at[q, chunk_rows(own)], dst_ref=ein.at[q, chunk_rows(own % 8)],
+                        send_sem=es.at[q, dx * 4 + dy], recv_sem=er.at[q, own % 8],
+                        device_id=(to[0], to[1], 1 - rep), device_id_type=MESH,
+                    )
+                )
+        return copies
+
     mine_rows = pl.ds(pl.multiple_of(rep * half, half), half)
     other_rows = pl.ds(pl.multiple_of((1 - rep) * half, half), half)
 
-    def exchange(q):
+    def finished(q):
         for dx, dy, slot in plane():
             source = (x + 4 - dx) % 4 * 4 + (y + 4 - dy) % 4
             arrived(cf.at[q, chunk_rows(source)], gr.at[q, slot])
-        send(cf.at[q, other_rows], ein.at[q], es.at[q], er.at[q], (row, col, 1 - rep))
+        for slot in range(8):
+            arrived(ein.at[q, chunk_rows(slot)], er.at[q, slot])
 
     products(0)
     x_pass_on(0)
     products(1)
+    normed_forward()
     z_send(0)
     x_pass_on(1)
+    normed_ready()
     couple(0)
     z_send(1)
+    couple(1)
     z_share(0)
-    couple(1)
+    z_share(1)
     gather(0)
-    z_share(1)
+    columns_out(0)
     gather(1)
-    exchange(0)
-    exchange(1)
+    columns_out(1)
+    finished(0)
+    finished(1)
     block = jnp.concatenate([cf[0, mine_rows, :], cf[1, mine_rows, :]], 1)
     s_out[mine_rows, :] = 0.5 * (block + block.T)
-    for q in range(2):
-        arrived(ein.at[q], er.at[q])
     mirrored = jnp.concatenate([ein[0].T, ein[1].T], 0)
     s_out[other_rows, :] = 0.5 * (jnp.concatenate([cf[0, other_rows, :], cf[1, other_rows, :]], 1) + mirrored)
     for copy, mine in first:
@@ -269,6 +354,12 @@
         @pl.when(jnp.logical_not(mine))
         def _():
             copy.wait_send()
+
+    @pl.when(crosses)
+    def _():
+        for q in range(2):
+            for copy in cross_copies(q):
+                copy.wait_send()
 
     for copy in sent:
         copy.wait_send()
@@ -295,11 +386,11 @@
             vmem((rows, columns), BF16),
             vmem((rows, columns), BF16),
             vmem((tile, width), F32),
-            vmem((width, width), F32),
+            vmem((4, width, part), F32),
             vmem((2, tile, part), F32),
-            vmem((width, tile), BF16),
-            vmem((width, tile), BF16),
-            vmem((2, columns, part), F32),
+            vmem((width, 4 * tile), BF16),
+            vmem((width, 4 * tile), BF16),
+            vmem((2, 8, 4, tile // 4, part), F32),
             vmem((2, columns, 2 * part), BF16),
             vmem((2, rows, part), F32),
             vmem((2, 2, 2 * tile, part), F32),
@@ -313,10 +404,18 @@
             vmem((2, 8, chunk, part), F32),
             vmem((2, width, part), F32),
             vmem((2, 2 * part, part), F32),
+            vmem((2, 8, tile // 4, part), F32),
+            vmem((4, 4, tile, part), F32),
             dma((16,)),
-            dma((2,)),
-            dma((2, 2)),
-            dma((2, 2)),
+            dma((5,)),
+            dma((2, 7)),
+            dma((2, 8)),
+            dma((3,)),
+            dma((4,)),
+            dma((3,)),
+            dma((4,)),
+            dma((2, 8)),
+            dma((2, 8)),
             dma((2, 3)),
             dma((2, 3)),
             dma((2, 6)),
@@ -329,10 +428,10 @@
             dma((2, 8)),
             dma((2, 15)),
             dma((2, 15)),
-            dma((2,)),
-            dma((2,)),
+            dma((2, 16)),
+            dma((2, 8)),
         ],
-        compiler_params=pltpu.CompilerParams(collective_id=0, has_side_effects=True, vmem_limit_bytes=48 * 1024 * 1024),
+        compiler_params=pltpu.CompilerParams(collective_id=0, has_side_effects=True, vmem_limit_bytes=60 * 1024 * 1024),
     )(tile_structure, ancestor_inverse, factor, factor_normalizer)
     return ancestor_columns, pivot_inverse - symmetric
 

time: 99.2 us -> 89.3 us (0.900)
  Pallas kernels: 93.9 us -> 83.5 us
  other arithmetic: 0.86 us -> 1.9 us
    pallas_call x1, Pallas kernels: 93.9 us -> 83.5 us  [body(): pl.pallas_call(kernel, out_shape=(jax.ShapeDtypeStruct((tile, 2 * part),...]
    sub x1, other arithmetic: 0.86 us -> 1.9 us  [body(): return (ancestor_columns, pivot_inverse - symmetric)]
    unnamed x8 -> x4, local copies, waits for them, and re-layouts: 3.59 us -> 2.98 us
where the time goes in v2:
time: 89.3 us; the launch traced here: 89 us
  Pallas kernels  83.5 us (94%)
  local copies, waits for them, and re-layouts  2.98 us (3%)
  other arithmetic  1.9 us (2%)
    pallas_call x1, Pallas kernels, body(): pl.pallas_call(kernel, out_shape=(jax.ShapeDtypeStruct((tile, 2 * part),...  83.5 us
    unnamed x4, local copies, waits for them, and re-layouts  2.98 us
    sub x1, other arithmetic, body(): return (ancestor_columns, pivot_inverse - symmetric)  1.9 us

profile of v2, /device:TPU:1, one launch (start us, length us, event | category | flops | bytes accessed | tf_op | source)
XLA Modules:
  0.0 89.0 jit_solution(1672892790993765543)
XLA Ops:
  0.6 0.0 copy-start
  0.6 1.4 %copy.7.tiles = s32[16,8]{1,0:T(8,128)} copy(s32[16,8]{0,1:T(8,128)} %param.6) | data formatting | bytes 1024 | tf_op args[1]
  2.1 83.5 %shard_map.68 = (f32[128,256]{1,0:T(8,128)}, f32[512,256]{1,0:T(8,128)}) custom-call(s32[16,8]{1,0:T(8,128)} %copy.7.tiles, f32[2048,1024]{1,0:T(8,128)} %a_hbm.1, f32[128,512]{1,0:T(8,128)} %f_hbm.1, f32[512,512]{1,0:T(8,128)} %n_hbm.1), custom_call_target="tpu_custom_call" | custom-call | tf_op jit(solution)/shard_map/pallas_call | solution.py:376
  85.6 0.0 copy-done
  85.6 1.9 %sub.3 = f32[512,256]{1,0:T(8,128)} subtract(f32[512,256]{1,0:T(8,128)S(1)} %copy-done, f32[512,256]{1,0:T(8,128)} %get-tuple-element.5) | non-fusion elementwise | flops 131072 | bytes 1572864 | tf_op jit(solution)/shard_map/sub | solution.py:436
  87.5 1.6 %copy.9 = f32[128,256]{1,0:T(8,128)} copy(f32[128,256]{1,0:T(8,128)} %get-tuple-element.8) | data formatting | bytes 262144
Async XLA Ops:
  0.6 84.9 %copy-start = (f32[512,256]{1,0:T(8,128)S(1)}, f32[512,256]{1,0:T(8,128)}, u32[]{:S(2)}) copy-start(f32[512,256]{1,0:T(8,128)} %param.9) | copy-start | bytes 1572868

commit v3 on v2

--- a/solution.py
+++ b/solution.py
@@ -170,36 +170,42 @@
 
     def mask_rows(a, carry):
         pltpu.make_async_copy(a_hbm.at[rows_of(a)], af.at[rows_of(a)], a_sem.at[a]).wait()
+        marks = tiles[pl.ds(a, 1), :]
         for b in range(8):
             columns = slice(b * tile, (b + 1) * tile)
-            high, low = split(af[rows_of(a), columns] * tiles[a, b].astype(F32))
+            high, low = split(af[rows_of(a), columns] * marks[:, b : b + 1])
             ah[rows_of(a), columns] = high
             al[rows_of(a), columns] = low
         return carry
 
     def y_exchange(q):
-        for slot in range(8):
-            arrived(xf.at[q, slot, y], s1r.at[q, slot])
-        for dy in (1, 3, 2):
-            send(xf.at[q, :, y], xf.at[q, :, y], ys.at[q, dy - 1], yr.at[q, dy - 1], place(x, (y + dy) % 4, z))
+        for group in range(2):
+            four = pl.ds(group * 4, 4)
+            for slot in range(4):
+                arrived(xf.at[q, group * 4 + slot, y], s1r.at[q, group * 4 + slot])
+            for dy in (1, 3, 2):
+                index = group * 3 + dy - 1
+                send(xf.at[q, four, y], xf.at[q, four, y], ys.at[q, index], yr.at[q, index], place(x, (y + dy) % 4, z))
 
     row_send(0)
     keep_transposed(0, value)
     for index in range(1, 4):
         keep_transposed(index, normed(index))
-    lax.fori_loop(0, 6, mask_rows, 0)
+    lax.fori_loop(0, 2, mask_rows, 0)
+    row_send(1)
+    lax.fori_loop(2, 7, mask_rows, 0)
     plane_send(0)
-    row_send(1)
-    lax.fori_loop(6, 12, mask_rows, 0)
+    lax.fori_loop(7, 13, mask_rows, 0)
+    plane_send(1)
     y_exchange(0)
-    lax.fori_loop(12, 16, mask_rows, 0)
-    plane_send(1)
+    lax.fori_loop(13, 16, mask_rows, 0)
     y_exchange(1)
     normed_share()
 
     def x_ready(q):
         for dy in range(1, 4):
-            arrived(xf.at[q, :, (y + 4 - dy) % 4], yr.at[q, dy - 1])
+            for group in range(2):
+                arrived(xf.at[q, pl.ds(group * 4, 4), (y + 4 - dy) % 4], yr.at[q, group * 3 + dy - 1])
         high, low = split(xf[q].reshape(8 * tile, part))
         xc[q, :, :part] = high
         xc[q, :, part:] = low
@@ -260,10 +266,16 @@
         return pl.ds(pl.multiple_of(index * chunk, chunk), chunk)
 
     def couple(q):
-        cp[q] = dot3((nth[...], ntl[...]), split(-zc[q]))
-        for dx, dy, slot in plane():
-            tx, ty = (x + dx) % 4, (y + dy) % 4
-            send(cp.at[q, chunk_rows(tx * 4 + ty)], win.at[q, slot], ws.at[q, slot], wr.at[q, slot], place(tx, ty, z))
+        sums = split(-zc[q])
+        for dx in (2, 1, 3, 0):
+            tx = (x + dx) % 4
+            rows = pl.ds(pl.multiple_of(tx * 4 * chunk, 4 * chunk), 4 * chunk)
+            cp[q, rows, :] = dot3((nth[rows, :], ntl[rows, :]), sums)
+            for dy in (2, 1, 3, 0):
+                if dx or dy:
+                    ty, slot = (y + dy) % 4, dx * 4 + dy - 1
+                    source = cp.at[q, chunk_rows(tx * 4 + ty)]
+                    send(source, win.at[q, slot], ws.at[q, slot], wr.at[q, slot], place(tx, ty, z))
 
     def columns_out(q):
         total = zc[q, rows_of(z_lo), :]
@@ -371,7 +383,7 @@
     rows, columns = ancestor_inverse.shape
     chunk = width // 16
     vmem, dma = pltpu.VMEM, pltpu.SemaphoreType.DMA
-    anywhere = pl.BlockSpec(memory_space=pl.ANY)
+    anywhere = pl.BlockSpec(memory_space=pltpu.HBM)
     in_vmem = pl.BlockSpec(memory_space=pltpu.VMEM)
     ancestor_columns, symmetric = pl.pallas_call(
         kernel,
@@ -379,7 +391,7 @@
             jax.ShapeDtypeStruct((tile, 2 * part), F32),
             jax.ShapeDtypeStruct((width, 2 * part), F32),
         ),
-        in_specs=[pl.BlockSpec(memory_space=pltpu.SMEM), anywhere, anywhere, anywhere],
+        in_specs=[in_vmem, anywhere, anywhere, anywhere],
         out_specs=(in_vmem, in_vmem),
         scratch_shapes=[
             vmem((rows, columns), F32),
@@ -416,8 +428,8 @@
             dma((4,)),
             dma((2, 8)),
             dma((2, 8)),
-            dma((2, 3)),
-            dma((2, 3)),
+            dma((2, 6)),
+            dma((2, 6)),
             dma((2, 6)),
             dma((2, 6)),
             dma((2, 3)),
@@ -431,8 +443,11 @@
             dma((2, 16)),
             dma((2, 8)),
         ],
-        compiler_params=pltpu.CompilerParams(collective_id=0, has_side_effects=True, vmem_limit_bytes=60 * 1024 * 1024),
-    )(tile_structure, ancestor_inverse, factor, factor_normalizer)
+        compiler_params=pltpu.CompilerParams(collective_id=0, has_side_effects=True, vmem_limit_bytes=40 * 1024 * 1024),
+    )(
+        tile_structure.astype(F32),
+        *(pltpu.with_memory_space_constraint(value, pltpu.HBM) for value in (ancestor_inverse, factor, factor_normalizer)),
+    )
     return ancestor_columns, pivot_inverse - symmetric
 
 

time: 89.3 us -> 84.9 us (0.951)
  local copies, waits for them, and re-layouts: 2.98 us -> 0.73 us
  Pallas kernels: 83.5 us -> 81.8 us
    unnamed x4 -> x3, local copies, waits for them, and re-layouts: 2.98 us -> 0.66 us
    pallas_call x1, Pallas kernels: 83.5 us -> 81.8 us  [body(): pl.pallas_call(kernel, out_shape=(jax.ShapeDtypeStruct((tile, 2 * part),...]
    sub x1, other arithmetic: 1.9 us -> 0.86 us  [body(): return (ancestor_columns, pivot_inverse - symmetric)]
where the time goes in v3:
time: 84.9 us; the launch traced here: 84.8 us
  Pallas kernels  81.8 us (96%)
  other arithmetic  1.61 us (2%)
    pallas_call x1, Pallas kernels, body(): pl.pallas_call(kernel, out_shape=(jax.ShapeDtypeStruct((tile, 2 * part),...  81.8 us

profile of v3, /device:TPU:1, one launch (start us, length us, event | category | flops | bytes accessed | tf_op | source)
XLA Modules:
  0.0 84.8 jit_solution(10756212045311395340)
XLA Ops:
  0.6 0.0 copy-start
  0.6 0.7 convert_element_type.3
  1.4 0.1 copy.8.tiles
  1.5 81.8 %shard_map.68 = (f32[128,256]{1,0:T(8,128)S(1)}, f32[512,256]{1,0:T(8,128)S(1)}) custom-call(f32[16,8]{1,0:T(8,128)S(1)} %copy.8.tiles, f32[2048,1024]{1,0:T(8,128)} %a_hbm.1, f32[128,512]{1,0:T(8,128)} %f_hbm.1, f32[512,512]{1,0:T(8,128)} %n_hbm.1), custom_call_target="tpu_custom_call" | custom-call | tf_op jit(solution)/shard_map/pallas_call | solution.py:388
  83.3 0.0 copy-done
  83.3 0.9 %sub.3 = f32[512,256]{1,0:T(8,128)} subtract(f32[512,256]{1,0:T(8,128)S(1)} %copy-done, f32[512,256]{1,0:T(8,128)S(1)} %get-tuple-element.5) | non-fusion elementwise | flops 131072 | bytes 1572864 | tf_op jit(solution)/shard_map/sub | solution.py:451
  84.2 0.7 copy.10
Async XLA Ops:
  0.6 82.7 %copy-start = (f32[512,256]{1,0:T(8,128)S(1)}, f32[512,256]{1,0:T(8,128)}, u32[]{:S(2)}) copy-start(f32[512,256]{1,0:T(8,128)} %param.9) | copy-start | bytes 1572868

commit v4 on v3

--- a/solution.py
+++ b/solution.py
@@ -248,19 +248,21 @@
         p[q, piece(xm, 1), :] += gin[q, 1]
         x_send(q, 5, xm, 1, xm, rin.at[q, 1, sides[1]])
 
-    def z_send(q):
+    def x_sum(q):
         arrived(rin.at[q, 0, sides[1]], xr.at[q, 2])
         arrived(rin.at[q, 1, sides[0]], xr.at[q, 3])
         arrived(rin.at[q, 0, sides[0]], xr.at[q, 4])
         arrived(rin.at[q, 1, sides[1]], xr.at[q, 5])
         for side in range(2):
             zc[q, sides[side]] = p[q, piece(x, side), :] + (rin[q, 0, sides[side]] + rin[q, 1, sides[side]])
+
+    def z_send(q):
         for dz in (2, 1, 3):
             to = (z_lo + dz) % 4
             send(zc.at[q, rows_of(to)], zin.at[q, dz - 1], zs.at[q, dz - 1], zr.at[q, dz - 1], place(x, y, z_hi * 4 + to))
 
     def plane():
-        return [(dx, dy, dx * 4 + dy - 1) for dx in range(4) for dy in range(4) if dx or dy]
+        return [(dx, dy, dx * 4 + dy - 1) for dx in (2, 1, 3, 0) for dy in (2, 1, 3, 0) if dx or dy]
 
     def chunk_rows(index):
         return pl.ds(pl.multiple_of(index * chunk, chunk), chunk)
@@ -317,8 +319,8 @@
 
     def cross_copies(q):
         copies = []
-        for dx in range(4):
-            for dy in range(4):
+        for dx in (2, 1, 3, 0):
+            for dy in (2, 1, 3, 0):
                 to = place((x + dx) % 4, (y + dy) % 4, z)
                 copies.append(
                     pltpu.make_async_remote_copy(
@@ -343,17 +345,19 @@
     x_pass_on(0)
     products(1)
     normed_forward()
+    x_sum(0)
     z_send(0)
     x_pass_on(1)
     normed_ready()
     couple(0)
-    z_send(1)
+    x_sum(1)
     couple(1)
     z_share(0)
     z_share(1)
+    z_send(1)
     gather(0)
+    gather(1)
     columns_out(0)
-    gather(1)
     columns_out(1)
     finished(0)
     finished(1)

time: 84.9 us -> 84.3 us (level)
  no operation moved by 1% of the time
where the time goes in v4:
time: 84.3 us; the launch traced here: 84.2 us
  Pallas kernels  81.2 us (96%)
  other arithmetic  1.61 us (2%)
    pallas_call x1, Pallas kernels, body(): pl.pallas_call(kernel, out_shape=(jax.ShapeDtypeStruct((tile, 2 * part),...  81.2 us

profile of v4, /device:TPU:1, one launch (start us, length us, event | category | flops | bytes accessed | tf_op | source)
XLA Modules:
  0.0 84.2 jit_solution(2000281994315180666)
XLA Ops:
  0.6 0.0 copy-start
  0.6 0.7 convert_element_type.3
  1.4 0.1 copy.8.tiles
  1.5 81.2 %shard_map.68 = (f32[128,256]{1,0:T(8,128)S(1)}, f32[512,256]{1,0:T(8,128)S(1)}) custom-call(f32[16,8]{1,0:T(8,128)S(1)} %copy.8.tiles, f32[2048,1024]{1,0:T(8,128)} %a_hbm.1, f32[128,512]{1,0:T(8,128)} %f_hbm.1, f32[512,512]{1,0:T(8,128)} %n_hbm.1), custom_call_target="tpu_custom_call" | custom-call | tf_op jit(solution)/shard_map/pallas_call | solution.py:392
  82.7 0.0 copy-done
  82.7 0.9 %sub.3 = f32[512,256]{1,0:T(8,128)} subtract(f32[512,256]{1,0:T(8,128)S(1)} %copy-done, f32[512,256]{1,0:T(8,128)S(1)} %get-tuple-element.5) | non-fusion elementwise | flops 131072 | bytes 1572864 | tf_op jit(solution)/shard_map/sub | solution.py:455
  83.6 0.7 copy.10
Async XLA Ops:
  0.6 82.1 %copy-start = (f32[512,256]{1,0:T(8,128)S(1)}, f32[512,256]{1,0:T(8,128)}, u32[]{:S(2)}) copy-start(f32[512,256]{1,0:T(8,128)} %param.9) | copy-start | bytes 1572868

commit v5 on v4

--- a/solution.py
+++ b/solution.py
@@ -354,8 +354,8 @@
     couple(1)
     z_share(0)
     z_share(1)
+    gather(0)
     z_send(1)
-    gather(0)
     gather(1)
     columns_out(0)
     columns_out(1)

time: 84.3 us -> 84.9 us (level)
  no operation moved by 1% of the time
where the time goes in v5:
time: 84.9 us; the launch traced here: 84.8 us
  Pallas kernels  81.8 us (96%)
  other arithmetic  1.61 us (2%)
    pallas_call x1, Pallas kernels, body(): pl.pallas_call(kernel, out_shape=(jax.ShapeDtypeStruct((tile, 2 * part),...  81.8 us

profile of v5, /device:TPU:1, one launch (start us, length us, event | category | flops | bytes accessed | tf_op | source)
XLA Modules:
  0.0 84.8 jit_solution(8012079321780189610)
XLA Ops:
  0.6 0.0 copy-start
  0.6 0.7 convert_element_type.3
  1.4 0.1 copy.8.tiles
  1.5 81.8 %shard_map.68 = (f32[128,256]{1,0:T(8,128)S(1)}, f32[512,256]{1,0:T(8,128)S(1)}) custom-call(f32[16,8]{1,0:T(8,128)S(1)} %copy.8.tiles, f32[2048,1024]{1,0:T(8,128)} %a_hbm.1, f32[128,512]{1,0:T(8,128)} %f_hbm.1, f32[512,512]{1,0:T(8,128)} %n_hbm.1), custom_call_target="tpu_custom_call" | custom-call | tf_op jit(solution)/shard_map/pallas_call | solution.py:392
  83.2 0.0 copy-done
  83.2 0.9 %sub.3 = f32[512,256]{1,0:T(8,128)} subtract(f32[512,256]{1,0:T(8,128)S(1)} %copy-done, f32[512,256]{1,0:T(8,128)S(1)} %get-tuple-element.5) | non-fusion elementwise | flops 131072 | bytes 1572864 | tf_op jit(solution)/shard_map/sub | solution.py:455
  84.1 0.7 copy.10
Async XLA Ops:
  0.6 82.6 %copy-start = (f32[512,256]{1,0:T(8,128)S(1)}, f32[512,256]{1,0:T(8,128)}, u32[]{:S(2)}) copy-start(f32[512,256]{1,0:T(8,128)} %param.9) | copy-start | bytes 1572868
